TPU v7x, 32 devices: a whole 2x2x4 slice. The times are simulated.
32 devices in a mesh: wide: 16 (over z, x, core), narrow: 2 (over y).
Axes of the slice: x: 2, y: 2, z: 4, core: 2. Of those that a mesh axis runs over, the one named last changes fastest.
Arguments:
- hess_inverse: bfloat16 [26880, 26880], P('wide', 'narrow'), may hold values from -0.0390625 to 0.0390625
- observations: bfloat16 [16, 26880], P('wide', 'narrow'), may hold values from -6 to 6
- adjoint_maps: bfloat16 [210, 2, 6144, 128], P('narrow', None, 'wide'), may hold values from -0.375 to 0.375
Outputs:
- estimate: float32 [6144, 210, 16], P(('wide', 'narrow'))
All inputs are finite; a program needn't handle non-finite values.
Results may differ from a plain program's by a relative error of at most 0.004.
Values may be sent and summed in bfloat16 or wider, within the bound.
A program may use at most 128 MiB of HBM per device.

v0:
```python
import functools
import math

import jax
import jax.numpy as jnp
import numpy as np
from jax import lax
from jax.experimental import pallas as pl
from jax.experimental.pallas import tpu as pltpu
from jax.sharding import PartitionSpec as P

MESH = pl.DeviceIdType.MESH
LANES = 128


def angles(freqs, times, turn):
    return 2.0 * math.pi * ((freqs * times) % turn) / turn


def analysis_table(nt, nf):
    a = angles(np.arange(nt)[:, None], np.arange(nf)[None, :], 2 * nf)
    return np.stack([np.cos(a), -np.sin(a)], axis=1).astype(np.float32)


def synthesis_table(nt, nf):
    a = angles(np.arange(nf)[:, None], np.arange(nt)[None, :], 2 * nf)
    return np.stack([np.cos(a), -np.sin(a)], axis=1).astype(np.float32)


def gather_kernel(zs, x_ref, out_ref, send, recv):
    w = lax.axis_index("wide")
    z, x, c = w // 4, (w // 2) % 2, w % 2

    def at(zz, xx, cc):
        return (zz * 2 + xx) * 2 + cc

    peers = [at((z + d) % zs, x, c) for d in range(1, zs)] + [at(z, 1 - x, c), at(z, x, 1 - c)]
    barrier = pltpu.get_barrier_semaphore()
    for p in peers:
        pl.semaphore_signal(barrier, inc=1, device_id={"wide": p}, device_id_type=MESH)
    pl.semaphore_wait(barrier, len(peers))

    copies = []

    def put(src, slot, k, target):
        cp = pltpu.make_async_remote_copy(
            src_ref=src, dst_ref=out_ref.at[slot], send_sem=send.at[k], recv_sem=recv.at[k],
            device_id={"wide": target}, device_id_type=MESH)
        cp.start()
        copies.append(cp)
        return cp

    along_z = [put(x_ref, w, d - 1, at((z + d) % zs, x, c)) for d in range(1, zs)]
    base_x = zs - 1
    base_c = base_x + zs
    along_x = [put(x_ref, w, base_x, at(z, 1 - x, c))]
    along_c = [put(x_ref, w, base_c, at(z, x, 1 - c))]
    out_ref[w] = x_ref[...]
    for d in range(1, zs):
        along_z[d - 1].wait_recv()
        slot = at((z + zs - d) % zs, x, c)
        along_x.append(put(out_ref.at[slot], slot, base_x + d, at(z, 1 - x, c)))
        along_c.append(put(out_ref.at[slot], slot, base_c + d, at(z, x, 1 - c)))
    for d in range(zs):
        along_x[d].wait_recv()
        slot = at((z + zs - d) % zs, 1 - x, c)
        along_c.append(put(out_ref.at[slot], slot, base_c + zs + d, at(z, x, 1 - c)))
    for cp in along_c:
        cp.wait_recv()
    for cp in copies:
        cp.wait_send()


def gather_wide(block, wide, ident):
    zs = wide // 4
    n = zs - 1 + zs + 2 * zs
    vm = pl.BlockSpec(memory_space=pltpu.VMEM)
    return pl.pallas_call(
        functools.partial(gather_kernel, zs),
        out_shape=jax.ShapeDtypeStruct((wide,) + block.shape, block.dtype),
        in_specs=[vm], out_specs=vm,
        scratch_shapes=[pltpu.SemaphoreType.DMA((n,)), pltpu.SemaphoreType.DMA((n,))],
        compiler_params=pltpu.CompilerParams(collective_id=ident, has_side_effects=True),
        name=f"gather{ident}",
    )(block)


def data_kernel(zs, parts, depth, obs_ref, hess_hbm, out_ref, hess, own32, mine, rows16, spread, wide_op, part, came,
                load, send, recv, send_n, recv_n):
    w, k = lax.axis_index("wide"), lax.axis_index("narrow")
    z, x, c = w // 4, (w // 2) % 2, w % 2
    step = hess.shape[0] // parts
    blocks = mine.shape[0]

    def at(zz, xx, cc):
        return (zz * 2 + xx) * 2 + cc

    def fetch(g):
        rows = pl.ds(pl.multiple_of(g * step, 16), step)
        return pltpu.make_async_copy(hess_hbm.at[rows], hess.at[rows], load.at[g])

    for g in range(parts):
        fetch(g).start()

    peers = [at((z + d) % zs, x, c) for d in range(1, zs)] + [at(z, 1 - x, c), at(z, x, 1 - c)]
    barrier = pltpu.get_barrier_semaphore()
    for p in peers:
        pl.semaphore_signal(barrier, inc=1, device_id={"wide": p}, device_id_type=MESH)
    pl.semaphore_signal(barrier, inc=1, device_id={"narrow": 1 - k}, device_id_type=MESH)
    for b in range(blocks):
        own32[b:b + 1, :] = obs_ref[0:1, b * LANES:(b + 1) * LANES].astype(jnp.float32)
    mine[...] = own32[...].astype(jnp.bfloat16)
    pl.semaphore_wait(barrier, len(peers) + 1)

    copies = []

    def put(src, slot, n, target):
        cp = pltpu.make_async_remote_copy(
            src_ref=src, dst_ref=rows16.at[slot], send_sem=send.at[n], recv_sem=recv.at[n],
            device_id={"wide": target}, device_id_type=MESH)
        cp.start()
        copies.append(cp)
        return cp

    base_x, base_c = zs - 1, 2 * zs - 1
    along_z = [put(mine, w, d - 1, at((z + d) % zs, x, c)) for d in range(1, zs)]
    along_x = [put(mine, w, base_x, at(z, 1 - x, c))]
    along_c = [put(mine, w, base_c, at(z, x, 1 - c))]

    def place(block, slot):
        spread[pl.ds(slot, blocks, stride=4 * zs), :] = block.astype(jnp.float32)

    place(mine[...], w)
    for d in range(1, zs):
        along_z[d - 1].wait_recv()
        slot = at((z + zs - d) % zs, x, c)
        along_x.append(put(rows16.at[slot], slot, base_x + d, at(z, 1 - x, c)))
        along_c.append(put(rows16.at[slot], slot, base_c + d, at(z, x, 1 - c)))
        place(rows16[slot], slot)
    for d in range(zs):
        along_x[d].wait_recv()
        slot = at((z + zs - d) % zs, 1 - x, c)
        along_c.append(put(rows16.at[slot], slot, base_c + zs + d, at(z, x, 1 - c)))
        place(rows16[slot], slot)
    for d in range(2 * zs):
        along_c[d].wait_recv()
        slot = at((z + zs - d) % zs, x, 1 - c) if d < zs else at((z + 2 * zs - d) % zs, 1 - x, 1 - c)
        place(rows16[slot], slot)
    scen = 4 * zs
    for b in range(blocks):
        wide_op[:, b * LANES:(b + 1) * LANES] = spread[b * scen:(b + 1) * scen, :].astype(jnp.bfloat16)

    def across(g):
        return pltpu.make_async_remote_copy(
            src_ref=part.at[g], dst_ref=came.at[g], send_sem=send_n.at[g], recv_sem=recv_n.at[g],
            device_id={"narrow": 1 - k}, device_id_type=MESH)

    def product(g, _):
        fetch(g).wait()
        rows = pl.ds(pl.multiple_of(g * step, 16), step)
        total = None
        for d in range(0, wide_op.shape[1], depth):
            term = lax.dot_general(
                wide_op[:, d:d + depth], hess[rows, d:d + depth], (((1,), (1,)), ((), ())),
                preferred_element_type=jnp.float32)
            total = term if total is None else total + term
        part[g] = total

        @pl.when(g > 0)
        def _():
            across(g - 1).start()
        return 0

    lax.fori_loop(0, parts, product, 0)
    for cp in copies:
        cp.wait_send()
    across(parts - 1).start()

    def gather(g, _):
        across(g).wait()
        out_ref[g] = part[g] + came[g]
        return 0

    lax.fori_loop(0, parts, gather, 0)


def data_product(observations, hess, wide, ident):
    rows, cols = hess.shape
    zs, blocks, parts = wide // 4, cols // LANES, 7
    depth = LANES * max(d for d in range(1, 17) if blocks % d == 0)
    n = zs - 1 + zs + 2 * zs
    vm = pl.BlockSpec(memory_space=pltpu.VMEM)
    f32, bf16, dma = jnp.float32, jnp.bfloat16, pltpu.SemaphoreType.DMA
    shape = (parts, wide, rows // parts)
    got = pl.pallas_call(
        functools.partial(data_kernel, zs, parts, depth),
        out_shape=jax.ShapeDtypeStruct(shape, f32),
        in_specs=[vm, pl.BlockSpec(memory_space=pltpu.HBM)], out_specs=vm,
        scratch_shapes=[
            pltpu.VMEM((rows, cols), bf16), pltpu.VMEM((blocks, LANES), f32), pltpu.VMEM((blocks, LANES), bf16),
            pltpu.VMEM((wide, blocks, LANES), bf16), pltpu.VMEM((wide * blocks, LANES), f32),
            pltpu.VMEM((wide, cols), bf16), pltpu.VMEM(shape, f32), pltpu.VMEM(shape, f32),
            dma((parts,)), dma((n,)), dma((n,)), dma((parts,)), dma((parts,)),
        ],
        compiler_params=pltpu.CompilerParams(
            collective_id=ident, has_side_effects=True, vmem_limit_bytes=56 << 20),
        name="data",
    )(observations, hess)
    return got.transpose(1, 0, 2).reshape(wide, rows)


def map_kernel(fs, groups, half, x_ref, a_hbm, out_ref, a, m32, sent, load, send, recv):
    k = lax.axis_index("narrow")
    other = 1 - k

    def fetch(g, side, h):
        rows = pl.ds(pl.multiple_of(h * half, 64), half)
        return pltpu.make_async_copy(
            a_hbm.at[pl.ds(g * fs, fs), :, rows], a.at[pl.ds(g * fs, fs), :, rows], load.at[side, g])

    for g in range(groups):
        fetch(g, 0, other).start()
    for g in range(groups):
        fetch(g, 1, k).start()

    barrier = pltpu.get_barrier_semaphore()
    pl.semaphore_signal(barrier, inc=1, device_id={"narrow": other}, device_id_type=MESH)
    pl.semaphore_wait(barrier, 1)

    m32[...] = jnp.zeros_like(m32)
    lane = lax.broadcasted_iota(jnp.int32, (8, LANES), 1)

    def chunk(g, h, dst):
        p0 = pl.multiple_of(h * half, 64)
        for i in range(fs):
            f = g * fs + i
            parts = []
            for c in range(2):
                head = a[f, c, pl.ds(p0, 128), :]
                tail = a[f, c, pl.ds(p0 + 128, 64), :]
                parts.append(jnp.concatenate([head, tail, tail], axis=0))
            got = lax.dot_general(
                x_ref[f], jnp.concatenate(parts, axis=1), (((1,), (1,)), ((), ())),
                preferred_element_type=jnp.float32)
            for c in range(2):
                low, high = got[c * 16:c * 16 + 8], got[c * 16 + 8:c * 16 + 16]
                rows = pl.ds(c * 16 + i, 8, stride=32)
                m32[0, rows, :] = low[:, :LANES]
                m32[1, rows, :] = high[:, :LANES]
                m32[2, rows, :] = jnp.where(lane < 64, low[:, LANES:], high[:, LANES:])
        for b in range(3):
            dst[:, :, b * LANES:(b + 1) * LANES] = m32[b].reshape(8, 32, LANES).astype(jnp.bfloat16)

    def across(g):
        return pltpu.make_async_remote_copy(
            src_ref=sent.at[g], dst_ref=out_ref.at[k, g], send_sem=send.at[g], recv_sem=recv.at[g],
            device_id={"narrow": other}, device_id_type=MESH)

    def first(g, _):
        fetch(g, 0, other).wait()
        chunk(g, other, sent.at[g])

        @pl.when(g > 0)
        def _():
            across(g - 1).start()
        return 0

    lax.fori_loop(0, groups, first, 0)

    def second(g, _):
        fetch(g, 1, k).wait()
        chunk(g, k, out_ref.at[k, g])

        @pl.when(g == 0)
        def _():
            across(groups - 1).start()
        return 0

    lax.fori_loop(0, groups, second, 0)

    def drain(g, _):
        across(g).wait()
        return 0

    lax.fori_loop(0, groups, drain, 0)


def apply_maps(x, maps, fs, ident):
    nf, _, points, sensors = maps.shape
    groups, half = nf // fs, points // 2
    vm = pl.BlockSpec(memory_space=pltpu.VMEM)
    return pl.pallas_call(
        functools.partial(map_kernel, fs, groups, half),
        out_shape=jax.ShapeDtypeStruct((2, groups, 8, 32, 2 * half), jnp.bfloat16),
        in_specs=[vm, pl.BlockSpec(memory_space=pltpu.HBM)], out_specs=vm,
        scratch_shapes=[
            pltpu.VMEM(maps.shape, jnp.bfloat16),
            pltpu.VMEM((3, 8 * 32, LANES), jnp.float32),
            pltpu.VMEM((groups, 8, 32, 2 * half), jnp.bfloat16),
            pltpu.SemaphoreType.DMA((2, groups)),
            pltpu.SemaphoreType.DMA((groups,)),
            pltpu.SemaphoreType.DMA((groups,)),
        ],
        compiler_params=pltpu.CompilerParams(
            collective_id=ident, has_side_effects=True, vmem_limit_bytes=48 << 20),
        name="maps",
    )(x, maps)


def time_kernel(scale, m_ref, table_ref, out_hbm, laid, sem):
    blocks, nt = m_ref.shape[0], laid.shape[2]

    def back(j, lanes):
        m = m_ref[:, j, :, lanes].reshape(blocks * 32, lanes.stop - lanes.start)
        got = lax.dot_general(m, table_ref[...], (((0,), (0,)), ((), ())), preferred_element_type=jnp.float32)
        return (got * scale)[:, :nt]

    def leave(n, rows):
        return pltpu.make_async_copy(laid.at[rows], out_hbm.at[rows], sem.at[n])

    first, second = leave(0, pl.ds(0, 128)), leave(1, pl.ds(128, 64))
    for j in range(8):
        got = back(j, slice(0, 256))
        laid[0:128, j, :] = got[0:128]
        laid[0:128, j + 8, :] = got[128:256]
    first.start()
    for j in range(8):
        got = back(j, slice(256, 384))
        laid[128:192, j, :] = got[0:64]
        laid[128:192, j + 8, :] = got[64:128]
    second.start()
    first.wait()
    second.wait()


def to_time(m, nt, nf, fs):
    blocks = m.shape[0] * m.shape[1]
    table = synthesis_table(nt, nf)
    laid = np.zeros((blocks, 2, 16, 256), np.float32)
    laid[:, :, :fs, :nt] = table.reshape(blocks, fs, 2, nt).transpose(0, 2, 1, 3)
    laid = laid.reshape(blocks * 32, 256)
    laid = laid.astype(jnp.bfloat16)
    vm = pl.BlockSpec(memory_space=pltpu.VMEM)
    return pl.pallas_call(
        functools.partial(time_kernel, 1.0 / nf),
        out_shape=jax.ShapeDtypeStruct((m.shape[4] // 2, 16, nt), jnp.float32),
        in_specs=[vm] * 2, out_specs=pl.BlockSpec(memory_space=pltpu.HBM),
        scratch_shapes=[pltpu.VMEM((m.shape[4] // 2, 16, nt), jnp.float32), pltpu.SemaphoreType.DMA((2,))],
        compiler_params=pltpu.CompilerParams(vmem_limit_bytes=32 << 20),
        name="time",
    )(m.reshape((blocks,) + m.shape[2:]), jnp.asarray(laid))


def per_device(wide, narrow, hess_inverse, observations, adjoint_maps):
    highest = lax.Precision.HIGHEST
    nf_dev, _, points, sensors = adjoint_maps.shape
    nf = nf_dev * narrow
    rows, cols = hess_inverse.shape
    nt = rows * wide // sensors
    scen = observations.shape[0] * wide
    sensors_dev = rows // nt
    fs = max([d for d in range(1, 17) if nf_dev % d == 0])
    tuned = (narrow == 2 and wide == 16 and scen == 16 and sensors == 128 and points == 384
             and cols % LANES == 0 and observations.shape[0] == 1 and rows % 112 == 0)
    table = jnp.asarray(analysis_table(nt, nf))
    if not tuned:
        observed = lax.all_gather(observations, "wide", axis=0, tiled=True)
        values = lax.dot_general(
            observed, hess_inverse, (((1,), (1,)), ((), ())), preferred_element_type=jnp.float32)
        values = values.reshape(scen, sensors_dev, nt)
        terms = jnp.einsum("nst,tcf->sfcn", values, table, precision=highest)
        spectra = lax.psum_scatter(terms, "narrow", scatter_dimension=1, tiled=True).astype(jnp.bfloat16)
        portion = lax.all_gather(spectra, "wide", axis=0, tiled=True)
        both = portion.transpose(1, 2, 3, 0)
        re, im = both[:, 0], both[:, 1]
        x = jnp.concatenate([jnp.concatenate([re, -im], 2), jnp.concatenate([im, re], 2)], 1)
        a = adjoint_maps.transpose(0, 2, 1, 3).reshape(nf_dev, points, 2 * sensors)
        m = jnp.einsum("frk,fpk->frp", x, a, preferred_element_type=jnp.float32).astype(jnp.bfloat16)
        m = m.reshape(nf_dev, 2, scen, points)
        m = lax.all_to_all(m, "narrow", split_axis=3, concat_axis=0, tiled=True)
        est = jnp.einsum("fcnp,fct->ptn", m.astype(jnp.float32), jnp.asarray(synthesis_table(nt, nf)),
                         precision=highest)
        return est * (1.0 / nf)
    values = data_product(observations, hess_inverse, wide, 0).reshape(scen, sensors_dev, nt)
    mine = lax.dynamic_slice_in_dim(table, lax.axis_index("narrow") * nf_dev, nf_dev, 2)
    spectra = jnp.einsum("nst,tcf->scnf", values, mine, precision=highest)
    spectra = spectra.reshape(-1, nf_dev).astype(jnp.bfloat16)
    full = gather_wide(spectra, wide, 1).reshape(sensors, 2, scen, nf_dev)
    both = full.transpose(3, 1, 2, 0)
    re, im = both[:, 0], both[:, 1]
    x = jnp.concatenate([jnp.concatenate([re, -im], 2), jnp.concatenate([im, re], 2)], 1)
    m = apply_maps(x, adjoint_maps, fs, 2)
    return to_time(m, nt, nf, fs).transpose(0, 2, 1)


def solution(mesh):
    wide, narrow = mesh.shape["wide"], mesh.shape["narrow"]
    return jax.shard_map(
        functools.partial(per_device, wide, narrow),
        mesh=mesh,
        in_specs=(P("wide", "narrow"), P("wide", "narrow"), P("narrow", None, "wide", None)),
        out_specs=P(("wide", "narrow"), None, None),
        check_vma=False,
    )
```

profile of v0, /device:TPU:0, one launch (start us, length us, event | category | flops | bytes accessed | tf_op | source)
XLA Modules:
  0.0 89.4 jit_solution(13378394867832097845)
XLA Ops:
  0.0 0.0 copy-start.1
  0.0 30.8 %data.1 = f32[7,16,240]{2,1,0:T(8,128)} custom-call(bf16[1,13440]{1,0:T(2,128)(2,1)} %obs_ref.1, bf16[1680,13440]{1,0:T(8,128)(2,1)} %hess_hbm.1), custom_call_target="tpu_custom_call" | custom-call | tf_op jit(solution)/shard_map/data/pallas_call | solution.py:195
  30.8 1.0 %copy.7 = f32[16,7,240]{2,1,0:T(8,128)S(1)} copy(f32[16,7,240]{2,0,1:T(8,128)} %bitcast.26) | data formatting | bytes 215040 | tf_op jit(solution)/shard_map/transpose | solution.py:209
  31.8 0.1 reshape_reshape.3
  31.9 0.0 copy-done.1
  31.9 0.4 fusion
  32.3 0.6 copy.9
  33.0 15.8 %gather1.1 = bf16[16,256,105]{2,1,0:T(8,128)(2,1)} custom-call(bf16[256,105]{1,0:T(8,128)(2,1)} %bitcast.27), custom_call_target="tpu_custom_call" | custom-call | tf_op jit(solution)/shard_map/gather1/pallas_call | solution.py:78
  48.8 2.5 %copy.10 = bf16[128,2,16,105]{0,2,3,1:T(8,128)(2,1)S(1)} copy(bf16[128,2,16,105]{3,2,1,0:T(8,128)(2,1)} %bitcast.25) | data formatting | bytes 1720320 | tf_op jit(solution)/shard_map/reshape | solution.py:388
  51.3 0.1 fusion.6
  51.4 0.1 slice_bitcast_fusion
  51.5 0.3 maximum_maximum_fusion.x_ref
  51.8 0.0 copy-start
  51.8 34.5 %maps.1 = bf16[2,7,8,32,384]{4,3,2,1,0:T(8,128)(2,1)S(1)} custom-call(bf16[105,32,256]{2,1,0:T(8,128)(2,1)S(1)} %maximum_maximum_fusion.x_ref, bf16[105,2,384,128]{3,2,1,0:T(8,128)(2,1)} %a_hbm.1), custom_call_target="tpu_custom_call" | custom-call | tf_op jit(solution)/shard_map/maps/pallas_call | solution.py:292
  86.3 0.0 copy-done
  86.3 3.0 %time.1 = f32[192,16,210]{2,1,0:T(8,128)} custom-call(bf16[14,8,32,384]{3,2,1,0:T(8,128)(2,1)S(1)} %bitcast.22, bf16[448,256]{1,0:T(8,128)(2,1)S(1)} %copy-done), custom_call_target="tpu_custom_call" | custom-call | tf_op jit(solution)/shard_map/time/pallas_call | solution.py:344
Async XLA Ops:
  0.0 31.9 %copy-start.1 = (f32[210,2,210]{2,0,1:T(8,128)S(1)}, f32[210,2,210]{2,0,1:T(8,128)}, u32[]{:S(2)}) copy-start(f32[210,2,210]{2,0,1:T(8,128)} %constant.14.clone) | copy-start | bytes 1058404
  51.8 34.5 %copy-start = (bf16[448,256]{1,0:T(8,128)(2,1)S(1)}, bf16[448,256]{1,0:T(8,128)(2,1)}, u32[]{:S(2)}) copy-start(bf16[448,256]{1,0:T(8,128)(2,1)} %constant.15.clone.table_ref) | copy-start | bytes 688132
where the time goes:
time: 89.6 us; the launch traced here: 89.4 us
  Pallas kernels  84.2 us (94%)
  local copies, waits for them, and re-layouts  4.4 us (5%)
    pallas_call x1, Pallas kernels, apply_maps(): pl.pallas_call(functools.partial(map_kernel, fs, groups, half), out_shape...  34.5 us
    pallas_call x1, Pallas kernels, data_product(): pl.pallas_call(functools.partial(data_kernel, zs, parts, depth), out_shap...  30.8 us
    pallas_call x1, Pallas kernels, gather_wide(): pl.pallas_call(functools.partial(gather_kernel, zs), out_shape=jax.ShapeD...  15.8 us
    pallas_call x1, Pallas kernels, to_time(): pl.pallas_call(functools.partial(time_kernel, 1.0 / nf), out_shape=jax.Sh...  3.03 us
    reshape x1, local copies, waits for them, and re-layouts, per_device(): full = gather_wide(spectra, wide, 1).reshape(sensors, 2, scen, nf_dev)  2.5 us

commit v1 on v0

v1 whole, which is shorter than its diff:
```python
import functools
import math

import jax
import jax.numpy as jnp
import numpy as np
from jax import lax
from jax.experimental import pallas as pl
from jax.experimental.pallas import tpu as pltpu
from jax.sharding import PartitionSpec as P

MESH = pl.DeviceIdType.MESH
LANES = 128
CHUNK = 256
GROUP = 16
EXTRA = 13
LEND = 4
STAGES = ((0, 2), (2, 2), (4, 2), (6, 1), (7, 1))


def angles(freqs, times, turn):
    return 2.0 * math.pi * ((freqs * times) % turn) / turn


def analysis_table(nt, nf):
    a = angles(np.arange(nt)[:, None], np.arange(nf)[None, :], 2 * nf)
    return np.stack([np.cos(a), -np.sin(a)], axis=1).astype(np.float32)


def synthesis_table(nt, nf):
    a = angles(np.arange(nf)[:, None], np.arange(nt)[None, :], 2 * nf)
    return np.stack([np.cos(a), -np.sin(a)], axis=1).astype(np.float32)


def layout(nf_dev):
    moved = nf_dev - EXTRA
    rest = moved % GROUP
    return [(moved, EXTRA, GROUP), (moved - rest, rest, 4 * -(-rest // 4))] + [
        (f, GROUP, GROUP) for f in range(0, moved - rest, GROUP)]


def main_kernel(zs, scen, nt, obs_ref, analysis_ref, synthesis_ref, hess_hbm, a_hbm, base_hbm, last_ref,
                table_out, hess, a, own32, mine, rows16, wide_op, part, came, series, gathered, flat, turned, m32, sent, m, laid,
                load, load_a, send_o, recv_o, send_n, recv_n, send_s, recv_s, send_m, recv_m, send_e, recv_e,
                leaving):
    w, k = lax.axis_index("wide"), lax.axis_index("narrow")
    z, x, c = w // 4, (w // 2) % 2, w % 2
    other = 1 - k
    slots_h, _, cols = hess.shape
    pieces, share, _ = mine.shape
    nf, _, points, sensors = a.shape
    half = points // 2
    rows = sensors // scen * nt
    full, rest = rows // CHUNK, rows % CHUNK
    local = rows // nt
    slots = layout(nf)
    moved = slots[0][0]
    groups = len(slots) - 2

    def at(zz, xx, cc):
        return (zz * 2 + xx) * 2 + cc

    def chunk_rows(g):
        return rest if isinstance(g, int) and g == full else CHUNK

    def fetch(g, size):
        lines = pl.ds(pl.multiple_of(g * CHUNK, 16), size)
        return pltpu.make_async_copy(hess_hbm.at[lines], hess.at[g % slots_h, pl.ds(0, size)], load.at[g])

    def side(h):
        return pl.ds(pl.multiple_of(h * half, 64), half)

    def fetch_a(n, own):
        f, size, _ = slots[n] if isinstance(n, int) else ((n - 2) * GROUP, GROUP, GROUP)
        freqs, place = pl.ds(f, size), side(k if own else other)
        return pltpu.make_async_copy(a_hbm.at[freqs, :, place], a.at[freqs, :, place], load_a.at[int(own), n])

    for g in range(slots_h):
        fetch(g, chunk_rows(g)).start()
    for n in [1, *range(2, groups + 2)]:
        fetch_a(n, False).start()

    near = [(dz, dx) for dx in (1, 0) for dz in [*range(1, zs), 0] if dz or dx]
    away = len(near)

    def target(i):
        dz, dx = near[i]
        return at((z + dz) % zs, (x + dx) % 2, c)

    def source(i, cc):
        dz, dx = near[i] if i < away else (0, 0)
        return at((z + zs - dz) % zs, (x + dx) % 2, cc)

    series[...] = jnp.zeros_like(series)
    part[...] = jnp.zeros_like(part)
    m[:, 1] = jnp.zeros_like(m[:, 1])
    barrier = pltpu.get_barrier_semaphore()
    for p in [target(i) for i in range(away)] + [at(z, x, 1 - c)]:
        pl.semaphore_signal(barrier, inc=1, device_id={"wide": p}, device_id_type=MESH)
    pl.semaphore_signal(barrier, inc=1, device_id={"narrow": other}, device_id_type=MESH)
    for b in range(pieces * share):
        own32[b:b + 1, :] = obs_ref[0:1, b * LANES:(b + 1) * LANES].astype(jnp.float32)
    for p in range(pieces):
        mine[p] = own32[p * share:(p + 1) * share].astype(jnp.bfloat16)
    pl.semaphore_wait(barrier, away + 2)

    def share_out(p, i):
        src, slot, dest = (mine.at[p], w, target(i)) if i < away else (
            rows16.at[source(i - away, c), p], source(i - away, c), at(z, x, 1 - c))
        if i == 2 * away:
            src = mine.at[p]
        return pltpu.make_async_remote_copy(
            src_ref=src, dst_ref=rows16.at[slot, p], send_sem=send_o.at[p, i], recv_sem=recv_o.at[p, i],
            device_id={"wide": dest}, device_id_type=MESH)

    for p in range(pieces):
        for i in range(away):
            share_out(p, i).start()
        share_out(p, 2 * away).start()

    def lend(e):
        freqs = pl.ds(moved + e, 1)
        return pltpu.make_async_remote_copy(
            src_ref=a_hbm.at[freqs, :, side(other)], dst_ref=a.at[freqs, :, side(k)],
            send_sem=send_e.at[e], recv_sem=recv_e.at[e], device_id={"narrow": other}, device_id_type=MESH)

    for e in range(LEND):
        lend(e).start()

    def relay(p):
        for i in range(away):
            share_out(p, i).wait_recv()
            share_out(p, away + i).start()

    def place(p, block, slot):
        flat[pl.ds(p * share * scen + slot, share, stride=scen), :] = block.astype(jnp.float32)

    def gather(p):
        place(p, mine[p], w)
        for i in range(away):
            place(p, rows16[source(i, c), p], source(i, c))
        for i in range(away + 1):
            share_out(p, away + i).wait_recv()
            place(p, rows16[source(i, 1 - c), p], source(i, 1 - c))
        for b in range(p * share, (p + 1) * share):
            wide_op[:, b * LANES:(b + 1) * LANES] = flat[b * scen:(b + 1) * scen, :].astype(jnp.bfloat16)

    def across(g):
        return pltpu.make_async_remote_copy(
            src_ref=part.at[g], dst_ref=came.at[g], send_sem=send_n.at[g], recv_sem=recv_n.at[g],
            device_id={"narrow": other}, device_id_type=MESH)

    def dot_rows(g, size, lanes):
        return lax.dot_general(
            wide_op[:, lanes], hess[g % slots_h, 0:size, lanes], (((1,), (1,)), ((), ())),
            preferred_element_type=jnp.float32)

    def product(g, size):
        fetch(g, size).wait()
        part[g, :, 0:size] = dot_rows(g, size, slice(0, cols))

    def merge(g):
        across(g).wait()
        at_lanes = pl.ds(pl.multiple_of(g * CHUNK, LANES), CHUNK)
        series[:, at_lanes] = part[g] + came[g]

    def transform(q):
        windows = []
        first, count = STAGES[q]
        for s in range(first, first + count):
            base = s * nt // LANES * LANES
            window = series[:, base:base + 3 * LANES]
            shift = s * nt - base
            if shift:
                window = pltpu.roll(window, 3 * LANES - shift, 1)
            windows.append(window[:, :2 * LANES])
        got = lax.dot_general(
            jnp.concatenate(windows, axis=0), analysis_ref[k], (((1,), (0,)), ((), ())),
            precision=lax.Precision.HIGHEST, preferred_element_type=jnp.float32).astype(jnp.bfloat16)
        for i in range(count):
            gathered[w * local + first + i, 0:scen] = got[i * scen:(i + 1) * scen, :LANES]
            gathered[w * local + first + i, scen:2 * scen] = got[i * scen:(i + 1) * scen, LANES:]

    def hand(q, i):
        slot, dest = (w, target(i)) if i < away else (source(i - away, c), at(z, x, 1 - c))
        lines = gathered.at[pl.ds(slot * local + STAGES[q][0], STAGES[q][1])]
        return pltpu.make_async_remote_copy(
            src_ref=lines, dst_ref=lines, send_sem=send_s.at[q, i], recv_sem=recv_s.at[q, i],
            device_id={"wide": dest}, device_id_type=MESH)

    def leave(q):
        for i in range(away):
            hand(q, i).start()
        hand(q, 2 * away).start()

    def hop(q):
        for i in range(away):
            hand(q, i).wait_recv()
            hand(q, away + i).start()

    early = 2
    for g in range(early):
        fetch(g, CHUNK).wait()
    relay(0)
    gather(0)
    for p in range(pieces):
        lanes = slice(p * share * LANES, (p + 1) * share * LANES)
        for g in range(early):
            part[g] = part[g] + dot_rows(g, CHUNK, lanes)
            if p + 1 < pieces:
                if g == 0:
                    relay(p + 1)
                if g == early - 1:
                    gather(p + 1)
    for g in range(early):
        fetch(g + slots_h, chunk_rows(g + slots_h)).start()
        across(g).start()
    lend(LEND).start()
    for p in range(pieces):
        for i in range(2 * away + 1):
            share_out(p, i).wait_send()

    def step(g, _):
        product(g, CHUNK)

        @pl.when(g + slots_h < full)
        def _():
            fetch(g + slots_h, CHUNK).start()

        @pl.when(g + slots_h == full)
        def _():
            fetch(full, rest).start()
            for n in [1, *range(2, groups + 2), 0]:
                fetch_a(n, True).start()

        @pl.when(g == 3)
        def _():
            merge(0)
            merge(1)
            transform(0)

        @pl.when(g == 4)
        def _():
            merge(2)

        @pl.when(g == 5)
        def _():
            merge(3)
            transform(1)

        across(g).start()
        lend(LEND + 1 + g - early).start()

        @pl.when(g == 3)
        def _():
            leave(0)

        @pl.when(g == 5)
        def _():
            leave(1)
            hop(0)
        return 0

    lax.fori_loop(early, full, step, 0)
    def finish(q):
        for i in range(away + 1):
            hand(q, away + i).wait_recv()

    def flatten(q):
        first, count = STAGES[q]
        for n in range(scen):
            block = gathered[n * local + first:n * local + first + count]
            start = (n * local + first) * 2 * scen
            flat[start:start + count * 2 * scen, :] = block.reshape(count * 2 * scen, LANES).astype(jnp.float32)

    product(full, rest)
    merge(full - 2)
    across(full).start()
    for e in range(LEND + 1 + full - early, nf - moved):
        lend(e).start()
    transform(2)
    merge(full - 1)
    leave(2)
    transform(3)
    hop(1)
    leave(3)
    height = turned.shape[0] // 32
    unit = (lax.broadcasted_iota(jnp.int32, (height, LANES), 0)
            == lax.broadcasted_iota(jnp.int32, (height, LANES), 1)).astype(jnp.float32).astype(jnp.bfloat16)
    m32[...] = jnp.zeros_like(m32)
    lane = lax.broadcasted_iota(jnp.int32, (8, LANES), 1)
    merge(full)
    transform(4)
    finish(0)
    leave(4)
    flatten(0)
    hop(2)
    finish(1)
    flatten(1)
    hop(3)
    finish(2)
    flatten(2)
    hop(4)
    finish(3)
    flatten(3)
    finish(4)
    flatten(4)

    def turn(n, _):
        both = jnp.concatenate([flat[pl.ds(2 * n + j, sensors, stride=32), :] for j in range(2)], axis=0)
        got = lax.dot_general(unit, both.astype(jnp.bfloat16), (((1,), (1,)), ((), ())),
                              preferred_element_type=jnp.float32)
        for j in range(2):
            turned[pl.ds(2 * n + j, height, stride=32), :] = got[:, j * LANES:(j + 1) * LANES]
        return 0

    lax.fori_loop(0, 16, turn, 0, unroll=4)

    def fill(n, h, dst, lent=False):
        f0, size, high = slots[n] if isinstance(n, int) else ((n - 2) * GROUP, GROUP, GROUP)
        p0 = pl.multiple_of(h * half, 64)
        for i in range(size):
            f = f0 + i
            at_x = nf + i if lent else f
            parts = []
            for e in range(2):
                start = a[f, e, pl.ds(p0, 128), :]
                end = a[f, e, pl.ds(p0 + 128, 64), :]
                parts.append(jnp.concatenate([start, end, end], axis=0))
            re = turned[pl.ds(pl.multiple_of(at_x * 32, 16), 16), :]
            im = turned[pl.ds(pl.multiple_of(at_x * 32 + 16, 16), 16), :]
            xs = jnp.concatenate([jnp.concatenate([re, -im], axis=1), jnp.concatenate([im, re], axis=1)], axis=0)
            got = lax.dot_general(
                xs.astype(jnp.bfloat16), jnp.concatenate(parts, axis=1), (((1,), (1,)), ((), ())),
                preferred_element_type=jnp.float32)
            for e in range(2):
                first, second = got[e * 16:e * 16 + 8], got[e * 16 + 8:e * 16 + 16]
                lines = pl.ds(e * high + i, 8, stride=2 * high)
                m32[0, lines, :] = first[:, :LANES]
                m32[1, lines, :] = second[:, :LANES]
                m32[2, lines, :] = jnp.where(lane < 64, first[:, LANES:], second[:, LANES:])
        for b in range(3):
            block = m32[b, 0:16 * high].reshape(8, 2 * high, LANES)
            dst[:, 0:2 * high, b * LANES:(b + 1) * LANES] = block.astype(jnp.bfloat16)

    def give(n):
        high = slots[n][2] if isinstance(n, int) else GROUP
        lines = pl.ds(0, 2 * high)
        dst = last_ref if isinstance(n, int) and n == groups + 1 else m.at[k, n, :, lines]
        return pltpu.make_async_remote_copy(
            src_ref=sent.at[n, :, lines], dst_ref=dst, send_sem=send_m.at[n], recv_sem=recv_m.at[n],
            device_id={"narrow": other}, device_id_type=MESH)

    def out_first(n, _):
        fetch_a(n, False).wait()
        fill(n, other, sent.at[n])

        @pl.when(n == 2)
        def _():
            give(1).start()

        @pl.when(n > 2)
        def _():
            give(n - 1).start()
        return 0

    fetch_a(1, False).wait()
    fill(1, other, sent.at[1])
    lax.fori_loop(2, groups + 2, out_first, 0)
    fetch_a(1, True).wait()
    fill(1, k, m.at[k, 1])
    give(groups + 1).start()

    def out_own(n, _):
        fetch_a(n, True).wait()
        fill(n, k, m.at[k, n])
        return 0

    lax.fori_loop(2, groups + 2, out_own, 0)
    fetch_a(0, True).wait()
    fill(0, k, m.at[k, 0])
    for e in range(nf - moved):
        lend(e).wait()
    fill(0, other, m.at[other, 0], lent=True)

    def back(which, size, add):
        def one(j, _):
            for lanes, p0 in ((slice(0, 2 * LANES), 0), (slice(2 * LANES, 3 * LANES), LANES)):
                wide = lanes.stop - lanes.start
                got = lax.dot_general(
                    m[which, 0:size, j, :, lanes].reshape(size * 32, wide), synthesis_ref[which, 0:size * 32],
                    (((0,), (0,)), ((), ())), preferred_element_type=jnp.float32)
                for u in range(2):
                    lines = pl.ds(pl.multiple_of((j + 8 * u) * half + p0, 64), wide // 2)
                    for ref, v in ((flat, 0), (turned, 1)):
                        value = got[u * (wide // 2):(u + 1) * (wide // 2), v * LANES:(v + 1) * LANES]
                        ref[lines, :] = ref[lines, :] + value if add else value
            return 0
        lax.fori_loop(0, 8, one, 0)

    back(k, groups + 2, False)
    give(1).wait()

    def drain(n, _):
        give(n).wait()
        return 0

    lax.fori_loop(2, groups + 1, drain, 0)
    back(other, groups + 1, True)
    table_out[...] = synthesis_ref[other, (groups + 1) * 32:(groups + 2) * 32]
    def lay(p, _):
        lines = pl.ds(p, 16, stride=half)
        laid[p, :, 0:LANES] = flat[lines, :]
        laid[p, :, LANES:nt] = turned[lines, :][:, :nt - LANES]
        return 0

    lax.fori_loop(0, half, lay, 0, unroll=4)
    out = pltpu.make_async_copy(laid, base_hbm, leaving)
    out.start()
    for q in range(len(STAGES)):
        for i in range(2 * away + 1):
            hand(q, i).wait_send()
    out.wait()
    give(groups + 1).wait()


def final_kernel(scale, base_hbm, last_hbm, table_hbm, out_hbm, laid, last_ref, table_ref, head, tail, load, sem):
    half, _, nt = out_hbm.shape
    part = half // 3

    def fetch(n):
        lines = pl.ds(n * part, part)
        return pltpu.make_async_copy(base_hbm.at[lines], laid.at[lines], load.at[n])

    def leave(n):
        lines = pl.ds(n * part, part)
        return pltpu.make_async_copy(laid.at[lines], out_hbm.at[lines], sem.at[n])

    small = [pltpu.make_async_copy(last_hbm, last_ref, load.at[3]), pltpu.make_async_copy(table_hbm, table_ref, load.at[4])]
    for cp in small:
        cp.start()
    for n in range(3):
        fetch(n).start()
    for cp in small:
        cp.wait()

    def last(j, lanes, p0):
        got = lax.dot_general(last_ref[j, :, lanes], table_ref[...], (((0,), (0,)), ((), ())),
                              preferred_element_type=jnp.float32)
        wide = (lanes.stop - lanes.start) // 2
        for u in range(2):
            start = (j + 8 * u) * half + p0
            head[start:start + wide] = got[u * wide:(u + 1) * wide, :LANES]
            tail[start:start + wide] = got[u * wide:(u + 1) * wide, LANES:]

    def lay(p, _):
        lines = pl.ds(p, 16, stride=half)
        laid[p, :, 0:LANES] = (laid[p, :, 0:LANES] + head[lines, :]) * scale
        laid[p, :, LANES:nt] = (laid[p, :, LANES:nt] + tail[lines, :][:, :nt - LANES]) * scale
        return 0

    for j in range(8):
        last(j, slice(0, 256), 0)
    for n in range(2):
        fetch(n).wait()
        lax.fori_loop(n * part, (n + 1) * part, lay, 0, unroll=8)
        leave(n).start()
    for j in range(8):
        last(j, slice(256, 384), 128)
    fetch(2).wait()
    lax.fori_loop(2 * part, half, lay, 0, unroll=8)
    leave(2).start()
    for n in range(3):
        leave(n).wait()


def estimate_of(observations, hess, maps, nt, nf, wide):
    rows, cols = hess.shape
    nf_dev, _, points, sensors = maps.shape
    zs, blocks, chunks, stages, pieces, ring = wide // 4, cols // LANES, -(-rows // CHUNK), len(STAGES), 3, 3
    half, n = points // 2, 2 * (2 * zs - 1) + 1
    slots = layout(nf_dev)
    moved = slots[0][0]
    whole = analysis_table(nt, nf).reshape(nt, 2, 2, nf_dev)
    analysis = np.zeros((2, 2 * LANES, 2, LANES), np.float32)
    for k in range(2):
        analysis[k, :nt, :, :nf_dev] = whole[:, :, k]
        analysis[k, :nt, :, nf_dev:nf_dev + EXTRA] = whole[:, :, 1 - k, moved:]
    analysis = analysis.reshape(2, 2 * LANES, 2 * LANES)
    table = synthesis_table(nt, nf).reshape(2, nf_dev, 2, nt)
    synthesis = np.zeros((2, len(slots), 32, 2 * LANES), np.float32)
    for i, (f, size, high) in enumerate(slots):
        for c in range(2):
            synthesis[:, i, c * high:c * high + size, :nt] = table[:, f:f + size, c]
    synthesis = synthesis.reshape(2, len(slots) * 32, 2 * LANES).astype(jnp.bfloat16)
    vm, hb = pl.BlockSpec(memory_space=pltpu.VMEM), pl.BlockSpec(memory_space=pltpu.HBM)
    f32, bf16, dma = jnp.float32, jnp.bfloat16, pltpu.SemaphoreType.DMA
    height = 8 * -(-(nf_dev + EXTRA) // 8)
    parts = pl.pallas_call(
        functools.partial(main_kernel, zs, wide, nt),
        out_shape=[jax.ShapeDtypeStruct((half, 16, nt), f32), jax.ShapeDtypeStruct((8, 32, points), bf16),
                   jax.ShapeDtypeStruct((32, 2 * LANES), bf16)],
        in_specs=[vm, vm, vm, hb, hb], out_specs=[hb, vm, vm],
        scratch_shapes=[
            pltpu.VMEM((ring, CHUNK, cols), bf16), pltpu.VMEM(maps.shape, bf16),
            pltpu.VMEM((blocks, LANES), f32), pltpu.VMEM((pieces, blocks // pieces, LANES), bf16),
            pltpu.VMEM((wide, pieces, blocks // pieces, LANES), bf16),
            pltpu.VMEM((wide, cols), bf16), pltpu.VMEM((chunks, wide, CHUNK), f32),
            pltpu.VMEM((chunks, wide, CHUNK), f32), pltpu.VMEM((wide, chunks * CHUNK), f32),
            pltpu.VMEM((sensors, 2 * wide, LANES), bf16), pltpu.VMEM((sensors * 2 * wide, LANES), f32),
            pltpu.VMEM((height * 32, LANES), f32), pltpu.VMEM((3, 16 * GROUP, LANES), f32),
            pltpu.VMEM((len(slots), 8, 32, points), bf16), pltpu.VMEM((2, len(slots), 8, 32, points), bf16),
            pltpu.VMEM((half, 16, nt), f32),
            dma((chunks,)), dma((2, len(slots))), dma((pieces, n)), dma((pieces, n)), dma((chunks,)), dma((chunks,)),
            dma((stages, n)), dma((stages, n)), dma((len(slots),)), dma((len(slots),)), dma((EXTRA,)), dma((EXTRA,)), dma(()),
        ],
        compiler_params=pltpu.CompilerParams(
            collective_id=0, has_side_effects=True, vmem_limit_bytes=60 << 20),
        name="main",
    )(observations, jnp.asarray(analysis), jnp.asarray(synthesis), hess, maps)
    return pl.pallas_call(
        functools.partial(final_kernel, 1.0 / nf),
        out_shape=jax.ShapeDtypeStruct((half, 16, nt), f32),
        in_specs=[hb] * 3, out_specs=hb,
        scratch_shapes=[pltpu.VMEM((half, 16, nt), f32), pltpu.VMEM((8, 32, points), bf16), pltpu.VMEM((32, 2 * LANES), bf16),
                        pltpu.VMEM((half * 16, LANES), f32),
                        pltpu.VMEM((half * 16, LANES), f32), dma((5,)), dma((3,))],
        compiler_params=pltpu.CompilerParams(vmem_limit_bytes=60 << 20),
        name="final",
    )(*parts)


def per_device(wide, narrow, hess_inverse, observations, adjoint_maps):
    highest = lax.Precision.HIGHEST
    nf_dev, _, points, sensors = adjoint_maps.shape
    nf = nf_dev * narrow
    rows, cols = hess_inverse.shape
    nt = rows * wide // sensors
    scen = observations.shape[0] * wide
    sensors_dev = rows // nt
    tuned = (narrow == 2 and wide == 16 and scen == 16 and sensors == 128 and points == 384
             and cols % LANES == 0 and observations.shape[0] == 1 and rows // CHUNK == 6 and sensors_dev == 8
             and cols // LANES % 3 == 0 and nf_dev == 105)
    table = jnp.asarray(analysis_table(nt, nf))
    if not tuned:
        observed = lax.all_gather(observations, "wide", axis=0, tiled=True)
        values = lax.dot_general(
            observed, hess_inverse, (((1,), (1,)), ((), ())), preferred_element_type=jnp.float32)
        values = values.reshape(scen, sensors_dev, nt)
        terms = jnp.einsum("nst,tcf->sfcn", values, table, precision=highest)
        spectra = lax.psum_scatter(terms, "narrow", scatter_dimension=1, tiled=True).astype(jnp.bfloat16)
        portion = lax.all_gather(spectra, "wide", axis=0, tiled=True)
        both = portion.transpose(1, 2, 3, 0)
        re, im = both[:, 0], both[:, 1]
        x = jnp.concatenate([jnp.concatenate([re, -im], 2), jnp.concatenate([im, re], 2)], 1)
        a = adjoint_maps.transpose(0, 2, 1, 3).reshape(nf_dev, points, 2 * sensors)
        m = jnp.einsum("frk,fpk->frp", x, a, preferred_element_type=jnp.float32).astype(jnp.bfloat16)
        m = m.reshape(nf_dev, 2, scen, points)
        m = lax.all_to_all(m, "narrow", split_axis=3, concat_axis=0, tiled=True)
        est = jnp.einsum("fcnp,fct->ptn", m.astype(jnp.float32), jnp.asarray(synthesis_table(nt, nf)),
                         precision=highest)
        return est * (1.0 / nf)
    return estimate_of(observations, hess_inverse, adjoint_maps, nt, nf, wide).transpose(0, 2, 1)


def solution(mesh):
    wide, narrow = mesh.shape["wide"], mesh.shape["narrow"]
    return jax.shard_map(
        functools.partial(per_device, wide, narrow),
        mesh=mesh,
        in_specs=(P("wide", "narrow"), P("wide", "narrow"), P("narrow", None, "wide", None)),
        out_specs=P(("wide", "narrow"), None, None),
        check_vma=False,
    )
```

time: 89.6 us -> 80.9 us (0.903)
  local copies, waits for them, and re-layouts: 4.4 us -> 0 us
  Pallas kernels: 84.2 us -> 80.7 us
    pallas_call x4 -> x2, Pallas kernels: 84.2 us -> 80.7 us  [the longest x1 75.6 us: estimate_of(): pl.pallas_call(functools.partial(main_kernel, zs, wide, nt), out_shape=[j...]
    reshape x1 -> x0, local copies, waits for them, and re-layouts: 2.5 us -> none  [per_device(): full = gather_wide(spectra, wide, 1).reshape(sensors, 2, scen, nf_dev)]
    transpose x1 -> x0, local copies, waits for them, and re-layouts: 0.97 us -> none  [data_product(): return got.transpose(1, 0, 2).reshape(wide, rows)]
where the time goes in v1:
time: 80.9 us; the launch traced here: 80.7 us
  Pallas kernels  80.7 us (100%)
    pallas_call x1, Pallas kernels, estimate_of(): pl.pallas_call(functools.partial(main_kernel, zs, wide, nt), out_shape=[j...  75.6 us
    pallas_call x1, Pallas kernels, estimate_of(): pl.pallas_call(functools.partial(final_kernel, 1.0 / nf), out_shape=jax.S...  5.1 us

profile of v1, /device:TPU:0, one launch (start us, length us, event | category | flops | bytes accessed | tf_op | source)
XLA Modules:
  0.0 80.7 jit_solution(13449592423188593360)
XLA Ops:
  0.0 75.6 %main.1 = (f32[192,16,210]{2,1,0:T(8,128)}, bf16[8,32,384]{2,1,0:T(8,128)(2,1)}, bf16[32,256]{1,0:T(8,128)(2,1)}) custom-call(bf16[1,13440]{1,0:T(2,128)(2,1)} %obs_ref.1, f32[2,256,256]{2,1,0:T(8,128)} %constant.4.clone.analysis_ref, bf16[2,224,256]{2,1,0:T(8,128)(2,1)} %constant.5.clone.synthesis_ref, bf16[1680,13440]{1,0:T(8,128)(2,1)} %hess_hbm.1, ...), custom_call_target="tpu_custom_call" | custom-call | tf_op jit(solution)/shard_map/main/pallas_call | solution.py:499
  75.6 5.1 %final.1 = f32[192,16,210]{2,1,0:T(8,128)} custom-call(f32[192,16,210]{2,1,0:T(8,128)} %get-tuple-element.8.base_hbm, bf16[8,32,384]{2,1,0:T(8,128)(2,1)} %get-tuple-element.9.last_hbm, bf16[32,256]{1,0:T(8,128)(2,1)} %get-tuple-element.10.table_hbm), custom_call_target="tpu_custom_call" | custom-call | tf_op jit(solution)/shard_map/final/pallas_call | solution.py:521

commit v2 on v1

--- a/solution.py
+++ b/solution.py
@@ -13,6 +13,7 @@
 LANES = 128
 CHUNK = 256
 GROUP = 16
+PITCH = 33
 EXTRA = 13
 LEND = 4
 STAGES = ((0, 2), (2, 2), (4, 2), (6, 1), (7, 1))
@@ -39,10 +40,10 @@
         (f, GROUP, GROUP) for f in range(0, moved - rest, GROUP)]
 
 
-def main_kernel(zs, scen, nt, obs_ref, analysis_ref, synthesis_ref, hess_hbm, a_hbm, base_hbm, last_ref,
-                table_out, hess, a, own32, mine, rows16, wide_op, part, came, series, gathered, flat, turned, m32, sent, m, laid,
+def main_kernel(zs, scen, nt, obs_hbm, analysis_hbm, synthesis_hbm, hess_hbm, a_hbm, base_hbm, last_ref, table_out,
+                obs_ref, analysis_ref, synthesis_ref, hess, a, own32, mine, rows16, wide_op, part, came, series, gathered, flat, turned, m32, sent, m, laid,
                 load, load_a, send_o, recv_o, send_n, recv_n, send_s, recv_s, send_m, recv_m, send_e, recv_e,
-                leaving):
+                leaving, load_t):
     w, k = lax.axis_index("wide"), lax.axis_index("narrow")
     z, x, c = w // 4, (w // 2) % 2, w % 2
     other = 1 - k
@@ -75,29 +76,36 @@
         freqs, place = pl.ds(f, size), side(k if own else other)
         return pltpu.make_async_copy(a_hbm.at[freqs, :, place], a.at[freqs, :, place], load_a.at[int(own), n])
 
+    near = [(dz, dx) for dx in (1, 0) for dz in [*range(1, zs), 0] if dz or dx]
+    away = len(near)
+
+    def target(i):
+        dz, dx = near[i]
+        return at((z + dz) % zs, (x + dx) % 2, c)
+
+    def source(i, cc):
+        dz, dx = near[i] if i < away else (0, 0)
+        return at((z + zs - dz) % zs, (x + dx) % 2, cc)
+
+    barrier = pltpu.get_barrier_semaphore()
+    for p in [target(i) for i in range(away)] + [at(z, x, 1 - c)]:
+        pl.semaphore_signal(barrier, inc=1, device_id={"wide": p}, device_id_type=MESH)
+    pl.semaphore_signal(barrier, inc=1, device_id={"narrow": other}, device_id_type=MESH)
+    read = [pltpu.make_async_copy(src, dst, load_t.at[i]) for i, (src, dst) in enumerate(
+        [(obs_hbm, obs_ref), (analysis_hbm, analysis_ref), (synthesis_hbm, synthesis_ref)])]
+    for cp in read:
+        cp.start()
+    series[...] = jnp.zeros_like(series)
+    part[...] = jnp.zeros_like(part)
+    for i in range(2):
+        m[i, 1, :, 2 * slots[1][2]:] = jnp.zeros_like(m[i, 1, :, 2 * slots[1][2]:])
+    m32[...] = jnp.zeros_like(m32)
+    for cp in read:
+        cp.wait()
     for g in range(slots_h):
         fetch(g, chunk_rows(g)).start()
     for n in [1, *range(2, groups + 2)]:
         fetch_a(n, False).start()
-
-    near = [(dz, dx) for dx in (1, 0) for dz in [*range(1, zs), 0] if dz or dx]
-    away = len(near)
-
-    def target(i):
-        dz, dx = near[i]
-        return at((z + dz) % zs, (x + dx) % 2, c)
-
-    def source(i, cc):
-        dz, dx = near[i] if i < away else (0, 0)
-        return at((z + zs - dz) % zs, (x + dx) % 2, cc)
-
-    series[...] = jnp.zeros_like(series)
-    part[...] = jnp.zeros_like(part)
-    m[:, 1] = jnp.zeros_like(m[:, 1])
-    barrier = pltpu.get_barrier_semaphore()
-    for p in [target(i) for i in range(away)] + [at(z, x, 1 - c)]:
-        pl.semaphore_signal(barrier, inc=1, device_id={"wide": p}, device_id_type=MESH)
-    pl.semaphore_signal(barrier, inc=1, device_id={"narrow": other}, device_id_type=MESH)
     for b in range(pieces * share):
         own32[b:b + 1, :] = obs_ref[0:1, b * LANES:(b + 1) * LANES].astype(jnp.float32)
     for p in range(pieces):
@@ -133,7 +141,7 @@
             share_out(p, away + i).start()
 
     def place(p, block, slot):
-        flat[pl.ds(p * share * scen + slot, share, stride=scen), :] = block.astype(jnp.float32)
+        flat[pl.ds(p * share * (scen + 1) + slot, share, stride=scen + 1), :] = block.astype(jnp.float32)
 
     def gather(p):
         place(p, mine[p], w)
@@ -143,7 +151,7 @@
             share_out(p, away + i).wait_recv()
             place(p, rows16[source(i, 1 - c), p], source(i, 1 - c))
         for b in range(p * share, (p + 1) * share):
-            wide_op[:, b * LANES:(b + 1) * LANES] = flat[b * scen:(b + 1) * scen, :].astype(jnp.bfloat16)
+            wide_op[:, b * LANES:(b + 1) * LANES] = flat[b * (scen + 1):b * (scen + 1) + scen, :].astype(jnp.bfloat16)
 
     def across(g):
         return pltpu.make_async_remote_copy(
@@ -212,8 +220,9 @@
                     relay(p + 1)
                 if g == early - 1:
                     gather(p + 1)
+            else:
+                fetch(g + slots_h, chunk_rows(g + slots_h)).start()
     for g in range(early):
-        fetch(g + slots_h, chunk_rows(g + slots_h)).start()
         across(g).start()
     lend(LEND).start()
     for p in range(pieces):
@@ -269,9 +278,8 @@
     def flatten(q):
         first, count = STAGES[q]
         for n in range(scen):
-            block = gathered[n * local + first:n * local + first + count]
-            start = (n * local + first) * 2 * scen
-            flat[start:start + count * 2 * scen, :] = block.reshape(count * 2 * scen, LANES).astype(jnp.float32)
+            for s in range(n * local + first, n * local + first + count):
+                flat[s * PITCH:s * PITCH + 2 * scen, :] = gathered[s].astype(jnp.float32)
 
     product(full, rest)
     merge(full - 2)
@@ -284,10 +292,9 @@
     transform(3)
     hop(1)
     leave(3)
-    height = turned.shape[0] // 32
+    height = turned.shape[0] // PITCH
     unit = (lax.broadcasted_iota(jnp.int32, (height, LANES), 0)
             == lax.broadcasted_iota(jnp.int32, (height, LANES), 1)).astype(jnp.float32).astype(jnp.bfloat16)
-    m32[...] = jnp.zeros_like(m32)
     lane = lax.broadcasted_iota(jnp.int32, (8, LANES), 1)
     merge(full)
     transform(4)
@@ -307,11 +314,11 @@
     flatten(4)
 
     def turn(n, _):
-        both = jnp.concatenate([flat[pl.ds(2 * n + j, sensors, stride=32), :] for j in range(2)], axis=0)
+        both = jnp.concatenate([flat[pl.ds(2 * n + j, sensors, stride=PITCH), :] for j in range(2)], axis=0)
         got = lax.dot_general(unit, both.astype(jnp.bfloat16), (((1,), (1,)), ((), ())),
                               preferred_element_type=jnp.float32)
         for j in range(2):
-            turned[pl.ds(2 * n + j, height, stride=32), :] = got[:, j * LANES:(j + 1) * LANES]
+            turned[pl.ds(2 * n + j, height, stride=PITCH), :] = got[:, j * LANES:(j + 1) * LANES]
         return 0
 
     lax.fori_loop(0, 16, turn, 0, unroll=4)
@@ -327,21 +334,22 @@
                 start = a[f, e, pl.ds(p0, 128), :]
                 end = a[f, e, pl.ds(p0 + 128, 64), :]
                 parts.append(jnp.concatenate([start, end, end], axis=0))
-            re = turned[pl.ds(pl.multiple_of(at_x * 32, 16), 16), :]
-            im = turned[pl.ds(pl.multiple_of(at_x * 32 + 16, 16), 16), :]
+            re = turned[pl.ds(at_x * PITCH, 16), :]
+            im = turned[pl.ds(at_x * PITCH + 16, 16), :]
             xs = jnp.concatenate([jnp.concatenate([re, -im], axis=1), jnp.concatenate([im, re], axis=1)], axis=0)
             got = lax.dot_general(
                 xs.astype(jnp.bfloat16), jnp.concatenate(parts, axis=1), (((1,), (1,)), ((), ())),
                 preferred_element_type=jnp.float32)
             for e in range(2):
                 first, second = got[e * 16:e * 16 + 8], got[e * 16 + 8:e * 16 + 16]
-                lines = pl.ds(e * high + i, 8, stride=2 * high)
+                lines = pl.ds(e * high + i, 8, stride=2 * high + 1)
                 m32[0, lines, :] = first[:, :LANES]
                 m32[1, lines, :] = second[:, :LANES]
                 m32[2, lines, :] = jnp.where(lane < 64, first[:, LANES:], second[:, LANES:])
         for b in range(3):
-            block = m32[b, 0:16 * high].reshape(8, 2 * high, LANES)
-            dst[:, 0:2 * high, b * LANES:(b + 1) * LANES] = block.astype(jnp.bfloat16)
+            for j in range(8):
+                block = m32[b, j * (2 * high + 1):j * (2 * high + 1) + 2 * high]
+                dst[j, 0:2 * high, b * LANES:(b + 1) * LANES] = block.astype(jnp.bfloat16)
 
     def give(n):
         high = slots[n][2] if isinstance(n, int) else GROUP
@@ -391,7 +399,7 @@
                     m[which, 0:size, j, :, lanes].reshape(size * 32, wide), synthesis_ref[which, 0:size * 32],
                     (((0,), (0,)), ((), ())), preferred_element_type=jnp.float32)
                 for u in range(2):
-                    lines = pl.ds(pl.multiple_of((j + 8 * u) * half + p0, 64), wide // 2)
+                    lines = pl.ds(p0 * 17 + j + 8 * u, wide // 2, stride=17)
                     for ref, v in ((flat, 0), (turned, 1)):
                         value = got[u * (wide // 2):(u + 1) * (wide // 2), v * LANES:(v + 1) * LANES]
                         ref[lines, :] = ref[lines, :] + value if add else value
@@ -409,7 +417,7 @@
     back(other, groups + 1, True)
     table_out[...] = synthesis_ref[other, (groups + 1) * 32:(groups + 2) * 32]
     def lay(p, _):
-        lines = pl.ds(p, 16, stride=half)
+        lines = pl.ds(p * 17, 16)
         laid[p, :, 0:LANES] = flat[lines, :]
         laid[p, :, LANES:nt] = turned[lines, :][:, :nt - LANES]
         return 0
@@ -449,12 +457,12 @@
                               preferred_element_type=jnp.float32)
         wide = (lanes.stop - lanes.start) // 2
         for u in range(2):
-            start = (j + 8 * u) * half + p0
-            head[start:start + wide] = got[u * wide:(u + 1) * wide, :LANES]
-            tail[start:start + wide] = got[u * wide:(u + 1) * wide, LANES:]
+            lines = pl.ds(p0 * 17 + j + 8 * u, wide, stride=17)
+            head[lines, :] = got[u * wide:(u + 1) * wide, :LANES]
+            tail[lines, :] = got[u * wide:(u + 1) * wide, LANES:]
 
     def lay(p, _):
-        lines = pl.ds(p, 16, stride=half)
+        lines = pl.ds(p * 17, 16)
         laid[p, :, 0:LANES] = (laid[p, :, 0:LANES] + head[lines, :]) * scale
         laid[p, :, LANES:nt] = (laid[p, :, LANES:nt] + tail[lines, :][:, :nt - LANES]) * scale
         return 0
@@ -477,7 +485,7 @@
 def estimate_of(observations, hess, maps, nt, nf, wide):
     rows, cols = hess.shape
     nf_dev, _, points, sensors = maps.shape
-    zs, blocks, chunks, stages, pieces, ring = wide // 4, cols // LANES, -(-rows // CHUNK), len(STAGES), 3, 3
+    zs, blocks, chunks, stages, pieces, ring = wide // 4, cols // LANES, -(-rows // CHUNK), len(STAGES), 3, 4
     half, n = points // 2, 2 * (2 * zs - 1) + 1
     slots = layout(nf_dev)
     moved = slots[0][0]
@@ -500,22 +508,23 @@
         functools.partial(main_kernel, zs, wide, nt),
         out_shape=[jax.ShapeDtypeStruct((half, 16, nt), f32), jax.ShapeDtypeStruct((8, 32, points), bf16),
                    jax.ShapeDtypeStruct((32, 2 * LANES), bf16)],
-        in_specs=[vm, vm, vm, hb, hb], out_specs=[hb, vm, vm],
+        in_specs=[hb] * 5, out_specs=[hb, vm, vm],
         scratch_shapes=[
+            pltpu.VMEM((1, cols), bf16), pltpu.VMEM(analysis.shape, f32), pltpu.VMEM(synthesis.shape, bf16),
             pltpu.VMEM((ring, CHUNK, cols), bf16), pltpu.VMEM(maps.shape, bf16),
             pltpu.VMEM((blocks, LANES), f32), pltpu.VMEM((pieces, blocks // pieces, LANES), bf16),
             pltpu.VMEM((wide, pieces, blocks // pieces, LANES), bf16),
             pltpu.VMEM((wide, cols), bf16), pltpu.VMEM((chunks, wide, CHUNK), f32),
             pltpu.VMEM((chunks, wide, CHUNK), f32), pltpu.VMEM((wide, chunks * CHUNK), f32),
-            pltpu.VMEM((sensors, 2 * wide, LANES), bf16), pltpu.VMEM((sensors * 2 * wide, LANES), f32),
-            pltpu.VMEM((height * 32, LANES), f32), pltpu.VMEM((3, 16 * GROUP, LANES), f32),
+            pltpu.VMEM((sensors, 2 * wide, LANES), bf16), pltpu.VMEM((sensors * PITCH, LANES), f32),
+            pltpu.VMEM((height * PITCH, LANES), f32), pltpu.VMEM((3, 8 * PITCH, LANES), f32),
             pltpu.VMEM((len(slots), 8, 32, points), bf16), pltpu.VMEM((2, len(slots), 8, 32, points), bf16),
             pltpu.VMEM((half, 16, nt), f32),
             dma((chunks,)), dma((2, len(slots))), dma((pieces, n)), dma((pieces, n)), dma((chunks,)), dma((chunks,)),
-            dma((stages, n)), dma((stages, n)), dma((len(slots),)), dma((len(slots),)), dma((EXTRA,)), dma((EXTRA,)), dma(()),
+            dma((stages, n)), dma((stages, n)), dma((len(slots),)), dma((len(slots),)), dma((EXTRA,)), dma((EXTRA,)), dma(()), dma((3,)),
         ],
         compiler_params=pltpu.CompilerParams(
-            collective_id=0, has_side_effects=True, vmem_limit_bytes=60 << 20),
+            collective_id=0, has_side_effects=True, vmem_limit_bytes=63 << 20),
         name="main",
     )(observations, jnp.asarray(analysis), jnp.asarray(synthesis), hess, maps)
     return pl.pallas_call(
@@ -523,8 +532,8 @@
         out_shape=jax.ShapeDtypeStruct((half, 16, nt), f32),
         in_specs=[hb] * 3, out_specs=hb,
         scratch_shapes=[pltpu.VMEM((half, 16, nt), f32), pltpu.VMEM((8, 32, points), bf16), pltpu.VMEM((32, 2 * LANES), bf16),
-                        pltpu.VMEM((half * 16, LANES), f32),
-                        pltpu.VMEM((half * 16, LANES), f32), dma((5,)), dma((3,))],
+                        pltpu.VMEM((half * 17, LANES), f32),
+                        pltpu.VMEM((half * 17, LANES), f32), dma((5,)), dma((3,))],
         compiler_params=pltpu.CompilerParams(vmem_limit_bytes=60 << 20),
         name="final",
     )(*parts)

time: 80.9 us -> 74.9 us (0.926)
  Pallas kernels: 80.7 us -> 74.3 us
    pallas_call x1, Pallas kernels: 75.6 us -> 71 us  [estimate_of(): pl.pallas_call(functools.partial(main_kernel, zs, wide, nt), out_shape=[j...]
    pallas_call x1, Pallas kernels: 5.1 us -> 3.35 us  [estimate_of(): pl.pallas_call(functools.partial(final_kernel, 1.0 / nf), out_shape=jax.S...]
where the time goes in v2:
time: 74.9 us; the launch traced here: 74.3 us
  Pallas kernels  74.3 us (99%)
    pallas_call x1, Pallas kernels, estimate_of(): pl.pallas_call(functools.partial(main_kernel, zs, wide, nt), out_shape=[j...  71 us
    pallas_call x1, Pallas kernels, estimate_of(): pl.pallas_call(functools.partial(final_kernel, 1.0 / nf), out_shape=jax.S...  3.35 us

profile of v2, /device:TPU:0, one launch (start us, length us, event | category | flops | bytes accessed | tf_op | source)
XLA Modules:
  0.0 74.3 jit_solution(14355758752838403122)
XLA Ops:
  0.0 71.0 %main.1 = (f32[192,16,210]{2,1,0:T(8,128)}, bf16[8,32,384]{2,1,0:T(8,128)(2,1)}, bf16[32,256]{1,0:T(8,128)(2,1)}) custom-call(bf16[1,13440]{1,0:T(2,128)(2,1)} %obs_hbm.1, f32[2,256,256]{2,1,0:T(8,128)} %constant.4.clone.analysis_hbm, bf16[2,224,256]{2,1,0:T(8,128)(2,1)} %constant.5.clone.synthesis_hbm, bf16[1680,13440]{1,0:T(8,128)(2,1)} %hess_hbm.1, ...), custom_call_target="tpu_custom_call" | custom-call | tf_op jit(solution)/shard_map/main/pallas_call | solution.py:507
  71.0 3.4 %final.1 = f32[192,16,210]{2,1,0:T(8,128)} custom-call(f32[192,16,210]{2,1,0:T(8,128)} %get-tuple-element.8.base_hbm, bf16[8,32,384]{2,1,0:T(8,128)(2,1)} %get-tuple-element.9.last_hbm, bf16[32,256]{1,0:T(8,128)(2,1)} %get-tuple-element.10.table_hbm), custom_call_target="tpu_custom_call" | custom-call | tf_op jit(solution)/shard_map/final/pallas_call | solution.py:530

commit v3 on v2

--- a/solution.py
+++ b/solution.py
@@ -100,8 +100,7 @@
     for i in range(2):
         m[i, 1, :, 2 * slots[1][2]:] = jnp.zeros_like(m[i, 1, :, 2 * slots[1][2]:])
     m32[...] = jnp.zeros_like(m32)
-    for cp in read:
-        cp.wait()
+    read[0].wait()
     for g in range(slots_h):
         fetch(g, chunk_rows(g)).start()
     for n in [1, *range(2, groups + 2)]:
@@ -182,9 +181,14 @@
             if shift:
                 window = pltpu.roll(window, 3 * LANES - shift, 1)
             windows.append(window[:, :2 * LANES])
-        got = lax.dot_general(
-            jnp.concatenate(windows, axis=0), analysis_ref[k], (((1,), (0,)), ((), ())),
-            precision=lax.Precision.HIGHEST, preferred_element_type=jnp.float32).astype(jnp.bfloat16)
+        whole = jnp.concatenate(windows, axis=0)
+        high = whole.astype(jnp.bfloat16)
+        low = (whole - high.astype(jnp.float32)).astype(jnp.bfloat16)
+        lines = count * scen
+        main = lax.dot_general(jnp.concatenate([high, low], axis=0), analysis_ref[k, 0], (((1,), (0,)), ((), ())),
+                               preferred_element_type=jnp.float32)
+        fine = lax.dot_general(high, analysis_ref[k, 1], (((1,), (0,)), ((), ())), preferred_element_type=jnp.float32)
+        got = (main[:lines] + (main[lines:] + fine)).astype(jnp.bfloat16)
         for i in range(count):
             gathered[w * local + first + i, 0:scen] = got[i * scen:(i + 1) * scen, :LANES]
             gathered[w * local + first + i, scen:2 * scen] = got[i * scen:(i + 1) * scen, LANES:]
@@ -270,6 +274,8 @@
             hop(0)
         return 0
 
+    for cp in read[1:]:
+        cp.wait()
     lax.fori_loop(early, full, step, 0)
     def finish(q):
         for i in range(away + 1):
@@ -434,7 +440,7 @@
 
 def final_kernel(scale, base_hbm, last_hbm, table_hbm, out_hbm, laid, last_ref, table_ref, head, tail, load, sem):
     half, _, nt = out_hbm.shape
-    part = half // 3
+    part = half // 6
 
     def fetch(n):
         lines = pl.ds(n * part, part)
@@ -444,10 +450,10 @@
         lines = pl.ds(n * part, part)
         return pltpu.make_async_copy(laid.at[lines], out_hbm.at[lines], sem.at[n])
 
-    small = [pltpu.make_async_copy(last_hbm, last_ref, load.at[3]), pltpu.make_async_copy(table_hbm, table_ref, load.at[4])]
+    small = [pltpu.make_async_copy(last_hbm, last_ref, load.at[6]), pltpu.make_async_copy(table_hbm, table_ref, load.at[7])]
     for cp in small:
         cp.start()
-    for n in range(3):
+    for n in range(6):
         fetch(n).start()
     for cp in small:
         cp.wait()
@@ -469,16 +475,12 @@
 
     for j in range(8):
         last(j, slice(0, 256), 0)
-    for n in range(2):
+        last(j, slice(256, 384), 128)
+    for n in range(6):
         fetch(n).wait()
         lax.fori_loop(n * part, (n + 1) * part, lay, 0, unroll=8)
         leave(n).start()
-    for j in range(8):
-        last(j, slice(256, 384), 128)
-    fetch(2).wait()
-    lax.fori_loop(2 * part, half, lay, 0, unroll=8)
-    leave(2).start()
-    for n in range(3):
+    for n in range(6):
         leave(n).wait()
 
 
@@ -495,6 +497,8 @@
         analysis[k, :nt, :, :nf_dev] = whole[:, :, k]
         analysis[k, :nt, :, nf_dev:nf_dev + EXTRA] = whole[:, :, 1 - k, moved:]
     analysis = analysis.reshape(2, 2 * LANES, 2 * LANES)
+    coarse = analysis.astype(jnp.bfloat16)
+    analysis = np.stack([coarse, (analysis - coarse.astype(np.float32)).astype(jnp.bfloat16)], axis=1)
     table = synthesis_table(nt, nf).reshape(2, nf_dev, 2, nt)
     synthesis = np.zeros((2, len(slots), 32, 2 * LANES), np.float32)
     for i, (f, size, high) in enumerate(slots):
@@ -510,7 +514,7 @@
                    jax.ShapeDtypeStruct((32, 2 * LANES), bf16)],
         in_specs=[hb] * 5, out_specs=[hb, vm, vm],
         scratch_shapes=[
-            pltpu.VMEM((1, cols), bf16), pltpu.VMEM(analysis.shape, f32), pltpu.VMEM(synthesis.shape, bf16),
+            pltpu.VMEM((1, cols), bf16), pltpu.VMEM(analysis.shape, bf16), pltpu.VMEM(synthesis.shape, bf16),
             pltpu.VMEM((ring, CHUNK, cols), bf16), pltpu.VMEM(maps.shape, bf16),
             pltpu.VMEM((blocks, LANES), f32), pltpu.VMEM((pieces, blocks // pieces, LANES), bf16),
             pltpu.VMEM((wide, pieces, blocks // pieces, LANES), bf16),
@@ -533,7 +537,7 @@
         in_specs=[hb] * 3, out_specs=hb,
         scratch_shapes=[pltpu.VMEM((half, 16, nt), f32), pltpu.VMEM((8, 32, points), bf16), pltpu.VMEM((32, 2 * LANES), bf16),
                         pltpu.VMEM((half * 17, LANES), f32),
-                        pltpu.VMEM((half * 17, LANES), f32), dma((5,)), dma((3,))],
+                        pltpu.VMEM((half * 17, LANES), f32), dma((8,)), dma((6,))],
         compiler_params=pltpu.CompilerParams(vmem_limit_bytes=60 << 20),
         name="final",
     )(*parts)

time: 74.9 us -> 74.6 us (level)
  no operation moved by 1% of the time
where the time goes in v3:
time: 74.6 us; the launch traced here: 74.1 us
  Pallas kernels  74.1 us (99%)
    pallas_call x1, Pallas kernels, estimate_of(): pl.pallas_call(functools.partial(main_kernel, zs, wide, nt), out_shape=[j...  70.7 us
    pallas_call x1, Pallas kernels, estimate_of(): pl.pallas_call(functools.partial(final_kernel, 1.0 / nf), out_shape=jax.S...  3.4 us

profile of v3, /device:TPU:0, one launch (start us, length us, event | category | flops | bytes accessed | tf_op | source)
XLA Modules:
  0.0 74.1 jit_solution(15594492719617940512)
XLA Ops:
  0.0 70.7 %main.1 = (f32[192,16,210]{2,1,0:T(8,128)}, bf16[8,32,384]{2,1,0:T(8,128)(2,1)}, bf16[32,256]{1,0:T(8,128)(2,1)}) custom-call(bf16[1,13440]{1,0:T(2,128)(2,1)} %obs_hbm.1, bf16[2,2,256,256]{3,2,1,0:T(8,128)(2,1)} %constant.4.clone.analysis_hbm, bf16[2,224,256]{2,1,0:T(8,128)(2,1)} %constant.5.clone.synthesis_hbm, bf16[1680,13440]{1,0:T(8,128)(2,1)} %hess_hbm.1, ...), custom_call_target="tpu_custom_call" | custom-call | tf_op jit(solution)/shard_map/main/pallas_call | solution.py:511
  70.7 3.4 %final.1 = f32[192,16,210]{2,1,0:T(8,128)} custom-call(f32[192,16,210]{2,1,0:T(8,128)} %get-tuple-element.8.base_hbm, bf16[8,32,384]{2,1,0:T(8,128)(2,1)} %get-tuple-element.9.last_hbm, bf16[32,256]{1,0:T(8,128)(2,1)} %get-tuple-element.10.table_hbm), custom_call_target="tpu_custom_call" | custom-call | tf_op jit(solution)/shard_map/final/pallas_call | solution.py:534
